TPU v7x, 128 devices: a whole 4x4x4 slice. The times are simulated.
128 devices in a mesh: row: 8 (over z_hi, y), col: 16 (over z_lo, x, core).
Axes of the slice: x: 4, y: 4, z: 4 (z_hi: 2, z_lo: 2; z = z_hi * 2 + z_lo), core: 2. Of those that a mesh axis runs over, the one named last changes fastest.
Arguments:
- features: bfloat16 [65536, 256], P(('col', 'row')), may hold values from -6 to 6
- weight: bfloat16 [256, 256], replicated, may hold values from -0.375 to 0.375
- bias: float32 [256], replicated, may hold values from -4 to 4
- cotangent: bfloat16 [65536, 256], P(('row', 'col')), may hold values from -6 to 6
- tiles: bfloat16 [8, 16, 384, 128, 128], P('row', 'col'), may hold values from -0.0546875 to 0.0546875
- tile_rows: int32 [8, 16, 384], P('row', 'col'), may hold values from 0 to 63, as said below
- tile_cols: int32 [8, 16, 384], P('row', 'col'), may hold values from 0 to 31
- tile_counts: int32 [8, 16], P('row', 'col'), may hold values from 24 to 384, as said below
Outputs:
- hidden: bfloat16 [65536, 256], P(('row', 'col'))
- grad_weight: float32 [256, 256], replicated
- grad_bias: float32 [256], replicated
- grad_features: bfloat16 [65536, 256], P(('col', 'row'))
Inputs may be any that keep to these rules, and one draw needn't show every extreme that they name: `tile_rows`: on each grid cell the slots name distinct blocks. `tile_counts`: slots at or after a cell's count are unused; some cell uses all 384 slots.
All inputs are finite; a program needn't handle non-finite values.
Results may differ from a plain program's by a relative error of at most 0.013.
Values may be sent and summed in bfloat16 or wider, within the bound.
A program may use at most 128 MiB of HBM per device.

v0:
```python
import math
import jax
import jax.numpy as jnp
from jax import lax
from jax.sharding import PartitionSpec as P


def accumulate(tiles, dest_ids, source_ids, live_count, source_blocks, out_blocks, backward):
    slots = tiles.shape[0]
    group = math.gcd(slots, 32)
    block = tiles.shape[-1]
    width = source_blocks.shape[-1]
    in_blocks = source_blocks.shape[0]
    flat_source = source_blocks.reshape(in_blocks, block * width)
    in_range = jnp.arange(in_blocks, dtype=jnp.int32)
    out_range = jnp.arange(out_blocks, dtype=jnp.int32)

    def one_group(step_index, total):
        start = step_index * group
        tile_group = lax.dynamic_slice_in_dim(tiles, start, group, 0)
        dest_group = lax.dynamic_slice_in_dim(dest_ids, start, group, 0)
        source_group = lax.dynamic_slice_in_dim(source_ids, start, group, 0)
        live = start + jnp.arange(group, dtype=jnp.int32) < live_count
        if backward:
            fetch_ids = dest_group
            target = source_group
        else:
            fetch_ids = source_group
            target = dest_group
        picker = (fetch_ids[:, None] == in_range[None, :]).astype(jnp.bfloat16)
        fetched = jnp.dot(picker, flat_source, preferred_element_type=jnp.float32)
        fetched = fetched.astype(jnp.bfloat16).reshape(group, block, width)
        if backward:
            contrib = jnp.einsum(
                "tji,tjf->tif", tile_group, fetched, preferred_element_type=jnp.float32
            )
        else:
            contrib = jnp.einsum(
                "tij,tjf->tif", tile_group, fetched, preferred_element_type=jnp.float32
            )
        placer = ((target[:, None] == out_range[None, :]) & live[:, None]).astype(jnp.float32)
        added = jnp.dot(
            placer.T,
            contrib.reshape(group, block * width),
            precision=lax.Precision.HIGHEST,
            preferred_element_type=jnp.float32,
        )
        return total + added

    start_total = jnp.zeros((out_blocks, block * width), jnp.float32)
    result = lax.fori_loop(0, slots // group, one_group, start_total)
    return result.reshape(out_blocks, block, width)


def per_device(features, weight, bias, cotangent, tiles, tile_rows, tile_cols, tile_counts):
    tile_set = tiles[0, 0]
    dest_ids = tile_rows[0, 0]
    source_ids = tile_cols[0, 0]
    live_count = tile_counts[0, 0]
    block = tile_set.shape[-1]
    own_nodes = features.shape[0]
    width = features.shape[1]
    row_count = lax.axis_size("row")
    col_count = lax.axis_size("col")
    blocks_down = own_nodes * col_count // block
    blocks_across = own_nodes * row_count // block
    factor = 1.0 / math.sqrt(own_nodes * row_count * col_count)
    panel = lax.all_gather(features, "row", axis=0, tiled=True)
    panel_blocks = panel.reshape(blocks_across, block, width)
    partial_value = accumulate(
        tile_set, dest_ids, source_ids, live_count, panel_blocks, blocks_down, False
    )
    term = partial_value.reshape(blocks_down * block, width)
    summed = lax.psum_scatter(term, "col", scatter_dimension=0, tiled=True)
    aggregated = summed.astype(jnp.bfloat16)
    preact = jnp.dot(aggregated, weight, preferred_element_type=jnp.float32) + bias
    hidden = jax.nn.silu(preact).astype(jnp.bfloat16)
    sigma = jax.nn.sigmoid(preact)
    slope = sigma * (1.0 + preact * (1.0 - sigma))
    grad_pre = (cotangent.astype(jnp.float32) * slope).astype(jnp.bfloat16)
    local_weight = jnp.einsum("nf,ng->fg", aggregated, grad_pre, preferred_element_type=jnp.float32)
    local_bias = jnp.sum(grad_pre.astype(jnp.float32), axis=0)
    grad_agg = jnp.dot(grad_pre, weight.T, preferred_element_type=jnp.float32).astype(jnp.bfloat16)
    grad_panel = lax.all_gather(grad_agg, "col", axis=0, tiled=True)
    grad_blocks = grad_panel.reshape(blocks_down, block, width)
    partial_back = accumulate(
        tile_set, dest_ids, source_ids, live_count, grad_blocks, blocks_across, True
    )
    term_back = partial_back.reshape(blocks_across * block, width)
    grad_features = lax.psum_scatter(
        term_back.astype(jnp.bfloat16), "row", scatter_dimension=0, tiled=True
    )
    grad_weight, grad_bias = lax.psum((local_weight, local_bias), ("row", "col"))
    grad_weight = grad_weight * factor
    grad_bias = grad_bias * factor
    return (hidden, grad_weight, grad_bias, grad_features)


def solution(mesh):
    in_specs = (
        P(("col", "row"), None),
        P(),
        P(),
        P(("row", "col"), None),
        P("row", "col", None, None, None),
        P("row", "col", None),
        P("row", "col", None),
        P("row", "col"),
    )
    out_specs = (P(("row", "col"), None), P(), P(), P(("col", "row"), None))
    return jax.shard_map(
        per_device, mesh=mesh, in_specs=in_specs, out_specs=out_specs, check_vma=False
    )
```

profile of v0, /device:TPU:0, one launch (start us, length us, event | category | flops | bytes accessed | tf_op | source)
XLA Modules:
  0.0 667.1 jit_solution(5247763881698745133)
XLA Ops:
  9.4 58.5 %all-gather.3.cloned.1.call-done = bf16[4096,256]{1,0:T(8,128)(2,1)} async-done(((bf16[512,256]{1,0:T(8,128)(2,1)}), bf16[4096,256]{1,0:T(8,128)(2,1)}) %all-gather.3.cloned.1.call-update) | async-done | bytes 2097168 | tf_op jit(solution)/shard_map/all_gather | solution.py:68
  70.7 196.6 %while.28 = (s32[]{:T(128)}, f32[64,32768]{1,0:T(8,128)}, s32[384]{0:T(512)S(1)}, s32[]{:T(128)}, bf16[384,128,128]{2,1,0:T(8,128)(2,1)}, /*index=5*/s32[384]{0:...) while((s32[]{:T(128)}, f32[64,32768]{1,0:T(8,128)}, ...), condition=%wide.region_1.0_spmd.clone, body=%wide.region_0.0_spmd.clone.sunk | while | flops 1146098688 | bytes 103810120 | solution.py:51
  77.4 6.5 convolution_add_fusion.5
  83.9 3.2 copy-done.2
  93.8 6.5 convolution_add_fusion.5
  100.3 3.2 copy-done.2
  110.1 6.5 convolution_add_fusion.5
  116.7 3.2 copy-done.2
  126.5 6.5 convolution_add_fusion.5
  133.1 3.2 copy-done.2
  142.9 6.5 convolution_add_fusion.5
  149.4 3.2 copy-done.2
  159.3 6.5 convolution_add_fusion.5
  165.8 3.2 copy-done.2
  175.7 6.5 convolution_add_fusion.5
  182.2 3.2 copy-done.2
  192.0 6.5 convolution_add_fusion.5
  198.6 3.2 copy-done.2
  208.4 6.5 convolution_add_fusion.5
  214.9 3.2 copy-done.2
  224.8 6.5 convolution_add_fusion.5
  231.3 3.2 copy-done.2
  241.2 6.5 convolution_add_fusion.5
  247.7 3.2 copy-done.2
  257.6 6.5 convolution_add_fusion.5
  264.1 3.2 copy-done.2
  267.3 9.2 %reshape_reshape.11 = f32[8192,256]{1,0:T(8,128)} reshape(f32[64,32768]{1,0:T(8,128)} %get-tuple-element.312) | data formatting | bytes 16777216 | tf_op jit(solution)/shard_map/reshape;reshape | solution.py:73
  276.6 73.4 %reduce-scatter.3.cloned.1.call-done = f32[512,256]{1,0:T(8,128)} async-done(((f32[8192,256]{1,0:T(8,128)}), f32[512,256]{1,0:T(8,128)}) %reduce-scatter.3.cloned.1.call-update) | async-done | bytes 524304 | tf_op jit(solution)/shard_map/reduce_scatter | solution.py:74
  353.4 16.7 %copy.12 = bf16[1,1,384,128,128]{3,4,2,1,0:T(8,128)(2,1)} copy(bf16[1,1,384,128,128]{4,3,2,1,0:T(8,128)(2,1)} %bitcast.60) | data formatting | bytes 25165824 | tf_op args[4]
  371.2 18.1 %all-gather.5.cloned.1.call-done = bf16[8192,256]{1,0:T(8,128)(2,1)} async-done(((bf16[512,256]{1,0:T(8,128)(2,1)}), bf16[8192,256]{1,0:T(8,128)(2,1)}) %all-gather.5.cloned.1.call-update) | async-done | bytes 4194320 | tf_op jit(solution)/shard_map/all_gather | solution.py:84
  389.2 7.4 %reshape_reshape.12 = bf16[64,32768]{1,0:T(8,128)(2,1)} reshape(bf16[8192,256]{1,0:T(8,128)(2,1)} %all-gather.5.cloned.1.call-done) | data formatting | bytes 8388608 | tf_op jit(solution)/shard_map/reshape;reshape | solution.py:14
  396.6 183.3 %while.29 = (s32[]{:T(128)}, f32[32,32768]{1,0:T(8,128)}, s32[384]{0:T(512)S(1)}, s32[]{:T(128)}, bf16[384,128,128]{1,2,0:T(8,128)(2,1)}, /*index=5*/s32[384]{0:...) while((s32[]{:T(128)}, f32[32,32768]{1,0:T(8,128)}, ...), condition=%wide.region_7.8_spmd.clone, body=%wide.region_6.7_spmd.clone.sunk | while | flops 808456256 | bytes 72352824 | solution.py:51
  405.3 4.7 convolution_add_fusion.6
  420.6 4.7 convolution_add_fusion.6
  435.8 4.7 convolution_add_fusion.6
  443.2 3.0 convolution_convert_fusion.6
  451.1 4.7 convolution_add_fusion.6
  458.5 3.0 convolution_convert_fusion.6
  466.4 4.7 convolution_add_fusion.6
  481.7 4.7 convolution_add_fusion.6
  496.9 4.7 convolution_add_fusion.6
  512.2 4.7 convolution_add_fusion.6
  527.5 4.7 convolution_add_fusion.6
  542.7 4.7 convolution_add_fusion.6
  558.0 4.7 convolution_add_fusion.6
  573.3 4.7 convolution_add_fusion.6
  584.7 69.3 %psum.15 = f32[256]{0:T(256)S(1)} all-reduce(f32[256]{0:T(256)S(1)} %get-tuple-element.405), channel_id=1, replica_groups=mesh['row'=8,'col'=16] {'row','col'}, use_global_device_ids=true, to_apply=%region_5.6 | all-reduce | flops 256 | bytes 2048 | tf_op jit(solution)/shard_map/psum | solution.py:93
  656.2 4.3 reduce-scatter.5.cloned.1.call-done
  (319 shorter events, 216.0 us)
Async XLA Ops:
  7.2 342.9 %copy-start = (bf16[256,256]{1,0:T(8,128)(2,1)S(1)}, bf16[256,256]{1,0:T(8,128)(2,1)}, u32[]{:S(2)}) copy-start(bf16[256,256]{1,0:T(8,128)(2,1)} %param.13) | copy-start | bytes 393220
  7.2 60.7 %all-gather.3.cloned.1.call-start = ((), (), s32[]{:S(2)}) async-start(), calls=%async_computation.2 | async-start | bytes 2359296 | tf_op jit(solution)/shard_map/all_gather | solution.py:68
  7.9 342.1 %reduce-scatter.3.cloned.1.call-start = ((), (), s32[]{:S(2)}) async-start(), calls=%async_computation.3 | async-start | bytes 8912896 | tf_op jit(solution)/shard_map/reduce_scatter | solution.py:74
  72.8 4.5 slice-start
  74.9 2.5 slice-start.1
  83.9 3.2 copy-start.2
  89.2 4.5 slice-start
  91.3 2.5 slice-start.1
  100.3 3.2 copy-start.2
  105.6 4.5 slice-start
  107.7 2.5 slice-start.1
  116.7 3.2 copy-start.2
  122.0 4.5 slice-start
  124.1 2.5 slice-start.1
  133.0 3.2 copy-start.2
  138.3 4.5 slice-start
  140.4 2.5 slice-start.1
  149.4 3.2 copy-start.2
  154.7 4.5 slice-start
  156.8 2.5 slice-start.1
  165.8 3.2 copy-start.2
  171.1 4.5 slice-start
  173.2 2.5 slice-start.1
  182.2 3.2 copy-start.2
  187.5 4.5 slice-start
  189.6 2.5 slice-start.1
  198.6 3.2 copy-start.2
  203.8 4.5 slice-start
  205.9 2.5 slice-start.1
  214.9 3.2 copy-start.2
  220.2 4.5 slice-start
  222.3 2.5 slice-start.1
  231.3 3.2 copy-start.2
  236.6 4.5 slice-start
  238.7 2.5 slice-start.1
  247.7 3.2 copy-start.2
  253.0 4.5 slice-start
  255.1 2.5 slice-start.1
  264.1 3.2 copy-start.2
  276.6 73.5 %copy-start.6 = (bf16[512,256]{1,0:T(8,128)(2,1)S(1)}, bf16[512,256]{1,0:T(8,128)(2,1)}, u32[]{:S(2)}) copy-start(bf16[512,256]{1,0:T(8,128)(2,1)} %param.15) | copy-start | bytes 786436
  276.6 73.5 %copy-start.7 = (f32[256]{0:T(256)S(1)}, f32[256]{0:T(256)}, u32[]{:S(2)}) copy-start(f32[256]{0:T(256)} %param.14) | copy-start | bytes 3076
  276.6 112.7 %all-gather.5.cloned.1.call-start = ((), (), s32[]{:S(2)}) async-start(), calls=%async_computation.5 | async-start | bytes 4456448 | tf_op jit(solution)/shard_map/all_gather | solution.py:84
  353.2 301.4 %all-reduce.2.cloned.1.call-start = ((), (), s32[]{:S(2)}) async-start(), calls=%async_computation.4 | async-start | bytes 524288 | tf_op jit(solution)/shard_map/psum | solution.py:93
  353.4 16.7 %copy-start.5 = (f32[512,256]{1,0:T(8,128)S(1)}, f32[512,256]{1,0:T(8,128)}, u32[]{:S(2)}) copy-start(f32[512,256]{1,0:T(8,128)} %reduce-scatter.3.cloned.1.call-done) | copy-start | bytes 1572868
  371.1 289.5 %reduce-scatter.5.cloned.1.call-start = ((), (), s32[]{:S(2)}) async-start(), calls=%async_computation.6 | async-start | bytes 2359296 | tf_op jit(solution)/shard_map/reduce_scatter | solution.py:90
  402.8 2.4 copy-start.3
  418.1 2.4 copy-start.3
  579.9 80.7 %copy-start.1 = (bf16[256,256]{1,0:T(8,128)(2,1)S(1)}, bf16[256,256]{1,0:T(8,128)(2,1)}, u32[]{:S(2)}) copy-start(bf16[256,256]{1,0:T(8,128)(2,1)} %param.13) | copy-start | bytes 393220
  (22 other events, 47.9 us)
Sparse Core Ops, SparseCore 0:
  10.4 57.4 all-gather.2
  276.7 73.2 reduce-scatter.2
  353.3 35.9 all-gather.4
  394.4 141.9 all-reduce.1
  584.8 75.7 reduce-scatter.4
where the time goes:
time: 669 us; the launch traced here: 667 us
  matrix products  231 us (35%)
  local copies, waits for them, and re-layouts  174 us (26%)
  waiting for transfers between devices  155 us (23%)
  blocking collectives  69.3 us (10%)
  other arithmetic  21.7 us (3%)
  between operations  13.8 us (2%)
    dot_general x24, matrix products, one_group(): jnp.dot(placer.T, contrib.reshape(group, block * width), precision=lax.Pr...  134 us
    while x168, local copies, waits for them, and re-layouts  132 us
    reduce_scatter x1, waiting for transfers between devices, per_device(): summed = lax.psum_scatter(term, 'col', scatter_dimension=0, tiled=True)  73.4 us
    psum x1, blocking collectives, per_device(): lax.psum((local_weight, local_bias), ('row', 'col'))  69.3 us
    all_gather x1, waiting for transfers between devices, per_device(): panel = lax.all_gather(features, 'row', axis=0, tiled=True)  58.5 us
    dot_general x24, matrix products, one_group(): fetched = jnp.dot(picker, flat_source, preferred_element_type=jnp.float32)  44.3 us
    dot_general x12, matrix products, one_group(): jnp.einsum('tij,tjf->tif', tile_group, fetched, preferred_element_type=jn...  25 us
    dot_general x12, matrix products, one_group(): jnp.einsum('tji,tjf->tif', tile_group, fetched, preferred_element_type=jn...  23.2 us
  transfers between devices with their start and end apart: 5, of which 4 were waited for; matrix products, arithmetic and copies ran while one was open for 29% of the time, Pallas kernels for 0%

commit v1 on v0

--- a/solution.py
+++ b/solution.py
@@ -3,6 +3,7 @@
 import jax.numpy as jnp
 from jax import lax
 from jax.sharding import PartitionSpec as P
+from jax.lax import all_to_all, axis_size
 
 
 def accumulate(tiles, dest_ids, source_ids, live_count, source_blocks, out_blocks, backward):
@@ -81,7 +82,9 @@
     local_weight = jnp.einsum("nf,ng->fg", aggregated, grad_pre, preferred_element_type=jnp.float32)
     local_bias = jnp.sum(grad_pre.astype(jnp.float32), axis=0)
     grad_agg = jnp.dot(grad_pre, weight.T, preferred_element_type=jnp.float32).astype(jnp.bfloat16)
-    grad_panel = lax.all_gather(grad_agg, "col", axis=0, tiled=True)
+    w1 = jnp.stack([grad_agg for _ in range(axis_size("col"))], axis=0)
+    extra = all_to_all(w1, "col", 0, 0)
+    grad_panel = jnp.concatenate(extra, axis=0)
     grad_blocks = grad_panel.reshape(blocks_down, block, width)
     partial_back = accumulate(
         tile_set, dest_ids, source_ids, live_count, grad_blocks, blocks_across, True

time: 669 us -> 697 us (1.042)
  waiting for transfers between devices: 155 us -> 176 us
    all_to_all x0 -> x1, waiting for transfers between devices: none -> 38.6 us  [per_device(): extra = all_to_all(w1, 'col', 0, 0)]
    all_gather x1 -> x0, waiting for transfers between devices: 18.1 us -> none  [per_device(): grad_panel = lax.all_gather(grad_agg, 'col', axis=0, tiled=True)]
  transfers between devices with their start and end apart: 5 -> 5, of which waited for: 4 -> 4; matrix products, arithmetic and copies ran while one was open for 29% -> 28% of each run, Pallas kernels for 0% -> 0%
where the time goes in v1:
time: 697 us; the launch traced here: 694 us
  matrix products  230 us (33%)
  local copies, waits for them, and re-layouts  177 us (25%)
  waiting for transfers between devices  176 us (25%)
  blocking collectives  70.1 us (10%)
  other arithmetic  21.7 us (3%)
  between operations  13.8 us (2%)
    dot_general x24, matrix products, one_group(): jnp.dot(placer.T, contrib.reshape(group, block * width), precision=lax.Pr...  134 us
    while x168, local copies, waits for them, and re-layouts  132 us
    reduce_scatter x1, waiting for transfers between devices, per_device(): summed = lax.psum_scatter(term, 'col', scatter_dimension=0, tiled=True)  73.4 us
    psum x1, blocking collectives, per_device(): lax.psum((local_weight, local_bias), ('row', 'col'))  70.1 us
    all_gather x1, waiting for transfers between devices, per_device(): panel = lax.all_gather(features, 'row', axis=0, tiled=True)  58.5 us
    dot_general x24, matrix products, one_group(): fetched = jnp.dot(picker, flat_source, preferred_element_type=jnp.float32)  44.4 us
    all_to_all x1, waiting for transfers between devices, per_device(): extra = all_to_all(w1, 'col', 0, 0)  38.6 us
    dot_general x12, matrix products, one_group(): jnp.einsum('tij,tjf->tif', tile_group, fetched, preferred_element_type=jn...  25 us
  transfers between devices with their start and end apart: 5, of which 4 were waited for; matrix products, arithmetic and copies ran while one was open for 28% of the time, Pallas kernels for 0%

profile of v1, /device:TPU:0, one launch (start us, length us, event | category | flops | bytes accessed | tf_op | source)
XLA Modules:
  0.0 694.5 jit_solution(3252629322665225685)
XLA Ops:
  9.4 58.5 %all-gather.2.cloned.1.call-done = bf16[4096,256]{1,0:T(8,128)(2,1)} async-done(((bf16[512,256]{1,0:T(8,128)(2,1)}), bf16[4096,256]{1,0:T(8,128)(2,1)}) %all-gather.2.cloned.1.call-update) | async-done | bytes 2097168 | tf_op jit(solution)/shard_map/all_gather | solution.py:69
  70.7 196.7 %while.28 = (s32[]{:T(128)}, f32[64,32768]{1,0:T(8,128)}, s32[384]{0:T(512)S(1)}, s32[]{:T(128)}, bf16[384,128,128]{2,1,0:T(8,128)(2,1)}, /*index=5*/s32[384]{0:...) while((s32[]{:T(128)}, f32[64,32768]{1,0:T(8,128)}, ...), condition=%wide.region_1.0_spmd.clone, body=%wide.region_0.0_spmd.clone.sunk | while | flops 1146098688 | bytes 103810120 | solution.py:52
  77.4 6.5 convolution_add_fusion.5
  83.9 3.2 copy-done.2
  93.8 6.5 convolution_add_fusion.5
  100.3 3.2 copy-done.2
  110.2 6.5 convolution_add_fusion.5
  116.7 3.2 copy-done.2
  126.6 6.5 convolution_add_fusion.5
  133.1 3.2 copy-done.2
  143.0 6.5 convolution_add_fusion.5
  149.5 3.2 copy-done.2
  159.4 6.5 convolution_add_fusion.5
  165.9 3.2 copy-done.2
  175.7 6.5 convolution_add_fusion.5
  182.3 3.2 copy-done.2
  192.1 6.5 convolution_add_fusion.5
  198.7 3.2 copy-done.2
  208.5 6.5 convolution_add_fusion.5
  215.0 3.2 copy-done.2
  224.9 6.5 convolution_add_fusion.5
  231.4 3.2 copy-done.2
  241.3 6.5 convolution_add_fusion.5
  247.8 3.2 copy-done.2
  257.7 6.5 convolution_add_fusion.5
  264.2 3.2 copy-done.2
  267.4 9.2 %reshape_reshape.8 = f32[8192,256]{1,0:T(8,128)} reshape(f32[64,32768]{1,0:T(8,128)} %get-tuple-element.312) | data formatting | bytes 16777216 | tf_op jit(solution)/shard_map/reshape;reshape | solution.py:74
  276.7 73.4 %reduce-scatter.3.cloned.1.call-done = f32[512,256]{1,0:T(8,128)} async-done(((f32[8192,256]{1,0:T(8,128)}), f32[512,256]{1,0:T(8,128)}) %reduce-scatter.3.cloned.1.call-update) | async-done | bytes 524304 | tf_op jit(solution)/shard_map/reduce_scatter | solution.py:75
  354.9 4.7 all-to-all-start
  359.7 16.7 %copy.12 = bf16[1,1,384,128,128]{3,4,2,1,0:T(8,128)(2,1)} copy(bf16[1,1,384,128,128]{4,3,2,1,0:T(8,128)(2,1)} %bitcast.60) | data formatting | bytes 25165824 | tf_op args[4]
  377.4 38.6 %all-to-all-done = bf16[16,512,256]{2,1,0:T(8,128)(2,1)} async-done(((bf16[16,512,256]{2,1,0:T(8,128)(2,1)}), bf16[16,512,256]{2,1,0:T(8,128)(2,1)}, u32[]{:S(2)}, u32[]{:S(2)}) %all-to-all-start) | async-done | bytes 4194336 | tf_op jit(solution)/shard_map/all_to_all | solution.py:86
  416.0 7.4 %reshape_reshape_reshape.3 = bf16[64,32768]{1,0:T(8,128)(2,1)} reshape(bf16[16,512,256]{2,1,0:T(8,128)(2,1)} %all-to-all-done) | data formatting | bytes 8388608 | tf_op jit(solution)/shard_map/reshape;reshape;reshape | solution.py:15
  423.4 183.1 %while.29 = (s32[]{:T(128)}, f32[32,32768]{1,0:T(8,128)}, s32[384]{0:T(512)S(1)}, s32[]{:T(128)}, bf16[384,128,128]{1,2,0:T(8,128)(2,1)}, /*index=5*/s32[384]{0:...) while((s32[]{:T(128)}, f32[32,32768]{1,0:T(8,128)}, ...), condition=%wide.region_7.8_spmd.clone, body=%wide.region_6.7_spmd.clone.sunk | while | flops 808456256 | bytes 72352824 | solution.py:52
  424.2 3.0 convolution_convert_fusion.6
  432.1 4.7 convolution_add_fusion.6
  447.4 4.7 convolution_add_fusion.6
  462.6 4.7 convolution_add_fusion.6
  477.9 4.7 convolution_add_fusion.6
  493.1 4.7 convolution_add_fusion.6
  508.4 4.7 convolution_add_fusion.6
  523.6 4.7 convolution_add_fusion.6
  538.9 4.7 convolution_add_fusion.6
  554.2 4.7 convolution_add_fusion.6
  569.4 4.7 convolution_add_fusion.6
  584.7 4.7 convolution_add_fusion.6
  599.9 4.7 convolution_add_fusion.6
  611.3 70.1 %psum.15 = f32[256]{0:T(256)S(1)} all-reduce(f32[256]{0:T(256)S(1)} %get-tuple-element.405), channel_id=1, replica_groups=mesh['row'=8,'col'=16] {'row','col'}, use_global_device_ids=true, to_apply=%region_5.6 | all-reduce | flops 256 | bytes 2048 | tf_op jit(solution)/shard_map/psum | solution.py:96
  683.7 4.3 reduce-scatter.5.cloned.1.call-done
  (319 shorter events, 220.2 us)
Async XLA Ops:
  7.2 343.0 %copy-start = (bf16[256,256]{1,0:T(8,128)(2,1)S(1)}, bf16[256,256]{1,0:T(8,128)(2,1)}, u32[]{:S(2)}) copy-start(bf16[256,256]{1,0:T(8,128)(2,1)} %param.13) | copy-start | bytes 393220
  7.2 60.7 %all-gather.2.cloned.1.call-start = ((), (), s32[]{:S(2)}) async-start(), calls=%async_computation.3 | async-start | bytes 2359296 | tf_op jit(solution)/shard_map/all_gather | solution.py:69
  7.9 342.2 %reduce-scatter.3.cloned.1.call-start = ((), (), s32[]{:S(2)}) async-start(), calls=%async_computation.4 | async-start | bytes 8912896 | tf_op jit(solution)/shard_map/reduce_scatter | solution.py:75
  72.8 4.5 slice-start
  74.9 2.5 slice-start.1
  83.9 3.2 copy-start.2
  89.2 4.5 slice-start
  91.3 2.5 slice-start.1
  100.3 3.2 copy-start.2
  105.6 4.5 slice-start
  107.7 2.5 slice-start.1
  116.7 3.2 copy-start.2
  122.0 4.5 slice-start
  124.1 2.5 slice-start.1
  133.1 3.2 copy-start.2
  138.4 4.5 slice-start
  140.5 2.5 slice-start.1
  149.5 3.2 copy-start.2
  154.8 4.5 slice-start
  156.9 2.5 slice-start.1
  165.9 3.2 copy-start.2
  171.2 4.5 slice-start
  173.3 2.5 slice-start.1
  182.3 3.2 copy-start.2
  187.6 4.5 slice-start
  189.7 2.5 slice-start.1
  198.6 3.2 copy-start.2
  204.0 4.5 slice-start
  206.0 2.5 slice-start.1
  215.0 3.2 copy-start.2
  220.3 4.5 slice-start
  222.4 2.5 slice-start.1
  231.4 3.2 copy-start.2
  236.7 4.5 slice-start
  238.8 2.5 slice-start.1
  247.8 3.2 copy-start.2
  253.1 4.5 slice-start
  255.2 2.5 slice-start.1
  264.2 3.2 copy-start.2
  276.7 73.5 %copy-start.6 = (bf16[512,256]{1,0:T(8,128)(2,1)S(1)}, bf16[512,256]{1,0:T(8,128)(2,1)}, u32[]{:S(2)}) copy-start(bf16[512,256]{1,0:T(8,128)(2,1)} %param.15) | copy-start | bytes 786436
  276.7 73.5 %copy-start.7 = (f32[256]{0:T(256)S(1)}, f32[256]{0:T(256)}, u32[]{:S(2)}) copy-start(f32[256]{0:T(256)} %param.14) | copy-start | bytes 3076
  354.9 61.1 %all-to-all-start = ((bf16[16,512,256]{2,1,0:T(8,128)(2,1)}), bf16[16,512,256]{2,1,0:T(8,128)(2,1)}, u32[]{:S(2)}, u32[]{:S(2)}) async-start(bf16[16,512,256]{2,1,0:T(8,128)(2,1)} %stack.2), calls=%async_computation.1 | async-start | bytes 8388608 | tf_op jit(solution)/shard_map/all_to_all | solution.py:86
  359.6 322.3 %all-reduce.2.cloned.1.call-start = ((), (), s32[]{:S(2)}) async-start(), calls=%async_computation.5 | async-start | bytes 524288 | tf_op jit(solution)/shard_map/psum | solution.py:96
  359.7 16.7 %copy-start.5 = (f32[512,256]{1,0:T(8,128)S(1)}, f32[512,256]{1,0:T(8,128)}, u32[]{:S(2)}) copy-start(f32[512,256]{1,0:T(8,128)} %reduce-scatter.3.cloned.1.call-done) | copy-start | bytes 1572868
  377.4 310.5 %reduce-scatter.5.cloned.1.call-start = ((), (), s32[]{:S(2)}) async-start(), calls=%async_computation.6 | async-start | bytes 2359296 | tf_op jit(solution)/shard_map/reduce_scatter | solution.py:93
  429.6 2.4 copy-start.3
  460.2 2.4 copy-start.3
  606.5 81.4 %copy-start.1 = (bf16[256,256]{1,0:T(8,128)(2,1)S(1)}, bf16[256,256]{1,0:T(8,128)(2,1)}, u32[]{:S(2)}) copy-start(bf16[256,256]{1,0:T(8,128)(2,1)} %param.13) | copy-start | bytes 393220
  (22 other events, 47.7 us)
Sparse Core Ops, SparseCore 0:
  10.3 57.4 all-gather.1
  276.8 73.2 reduce-scatter.2
  377.5 159.8 all-reduce.1
  611.5 76.4 reduce-scatter.4
